TPU v7x, 128 devices: a whole 4x4x4 slice. The times are simulated.
128 devices in a mesh: dev: 128 (over x, z, y, core).
Axes of the slice: x: 4, y: 4, z: 4, core: 2. Of those that a mesh axis runs over, the one named last changes fastest.
Arguments:
- saved: bfloat16 [128, 1024, 768], P('dev'), may hold values from -6 to 6
- cotangent: bfloat16 [128, 1024, 2048], P('dev'), may hold values from -6 to 6
- weights: bfloat16 [128, 768, 2048], P('dev'), may hold values from -0.21875 to 0.21875
- counts: int32 [64], replicated, may hold values from 1 to 8, as said below
- live_rows: int32 [128], P('dev'), may hold values from 1 to 1024, 81920 in all
- next_map: int32 [128], replicated, may hold values from 0 to 63, as said below
- master: float32 [64, 768, 2048], P(None, 'dev'), may hold values from -0.21875 to 0.21875
- moment1: bfloat16 [64, 768, 2048], P(None, 'dev'), may hold values from -6 to 6
- moment2: bfloat16 [64, 768, 2048], P(None, 'dev'), may hold values from 0.049804688 to 4
Outputs:
- input_grads: bfloat16 [128, 1024, 768], P('dev')
- master_out: float32 [64, 768, 2048], P(None, 'dev')
- moment1_out: bfloat16 [64, 768, 2048], P(None, 'dev')
- moment2_out: bfloat16 [64, 768, 2048], P(None, 'dev')
- next_weights: bfloat16 [128, 768, 2048], P('dev')
Inputs may be any that keep to these rules, and one draw needn't show every extreme that they name: The counts sum to 128; in the current placement expert e holds the counts[e] slots that follow those of experts below e; some expert has exactly 8 replicas. `next_map`: every expert is named by 1 to 8 slots; some expert by exactly 8. `live_rows`: the live rows of all slots sum to 81920, and some slot has exactly 1024.
All inputs are finite; a program needn't handle non-finite values. No bound on the sum of `live_rows` on one device may be relied on, other than what follows from the above.
Results may differ from a plain program's by a relative error of at most 0.0058.
Values may be sent and summed in bfloat16 or wider, within the bound.
No kernel may reach another device: no remote copies, remote signals or barrier semaphores. Data moves between devices by JAX's collectives and lax.ppermute only.
A program may use at most 128 MiB of HBM per device.

v0:
```python
import jax
import jax.numpy as jnp
from jax import lax
from jax.sharding import PartitionSpec as P

LEARN_RATE = 0.001
DECAY_RATE = 0.1
BETA_ONE = 0.9
BETA_TWO = 0.95
BIAS_ONE = 1.0 - 0.9**20
BIAS_TWO = 1.0 - 0.95**20
EPSILON = 1e-08


def contract_rows(left, right):
    return lax.dot_general(
        left, right, (((0,), (0,)), ((), ())), preferred_element_type=jnp.float32
    )


def contract_cols(left, right):
    return lax.dot_general(
        left, right, (((1,), (1,)), ((), ())), preferred_element_type=jnp.float32
    )


def per_device(saved, cotangent, weights, counts, live_rows, next_map, master, moment1, moment2):
    hidden_rows = saved[0]
    cot_rows = cotangent[0]
    slot_weights = weights[0]
    live_count = live_rows[0]
    row_count = hidden_rows.shape[0]
    devices = lax.axis_size("dev")
    expert_count, share_rows, model_width = master.shape
    row_index = jnp.arange(row_count, dtype=jnp.int32)
    masked = jnp.where((row_index < live_count)[:, None], cot_rows, jnp.zeros_like(cot_rows))
    input_grads = contract_cols(masked, slot_weights).astype(jnp.bfloat16)
    weight_sum = contract_rows(hidden_rows, masked)
    slot_grads = weight_sum.astype(jnp.bfloat16)
    slot_index = jnp.arange(devices, dtype=jnp.int32)
    bounds = jnp.cumsum(counts)
    holders = jnp.sum((bounds[None, :] <= slot_index[:, None]).astype(jnp.int32), axis=1)
    selector = (jnp.arange(expert_count, dtype=jnp.int32)[:, None] == holders[None, :]).astype(
        jnp.bfloat16
    )
    received = lax.all_to_all(slot_grads, "dev", split_axis=0, concat_axis=0, tiled=True)
    columns = received.shape[1]
    pieces = received.reshape(devices, share_rows, columns)
    expert_grads = jnp.einsum("es,src->erc", selector, pieces, preferred_element_type=jnp.float32)
    first_moment = BETA_ONE * moment1.astype(jnp.float32) + (1.0 - BETA_ONE) * expert_grads
    second_moment = (
        BETA_TWO * moment2.astype(jnp.float32) + (1.0 - BETA_TWO) * expert_grads * expert_grads
    )
    update = (
        first_moment / BIAS_ONE / (jnp.sqrt(second_moment / BIAS_TWO) + EPSILON)
        + DECAY_RATE * master
    )
    master_out = master - LEARN_RATE * update
    outgoing = jnp.take(master_out.astype(jnp.bfloat16), next_map, axis=0).reshape(
        devices * share_rows, model_width
    )
    arriving = lax.all_to_all(outgoing, "dev", split_axis=0, concat_axis=0, tiled=True)
    return (
        input_grads[None],
        master_out,
        first_moment.astype(jnp.bfloat16),
        second_moment.astype(jnp.bfloat16),
        arriving[None],
    )


def solution(mesh):
    placed = (
        P("dev", None, None),
        P("dev", None, None),
        P("dev", None, None),
        P(),
        P("dev"),
        P(),
        P(None, "dev", None),
        P(None, "dev", None),
        P(None, "dev", None),
    )
    return jax.shard_map(
        per_device,
        mesh=mesh,
        in_specs=placed,
        out_specs=(
            P("dev", None, None),
            P(None, "dev", None),
            P(None, "dev", None),
            P(None, "dev", None),
            P("dev", None, None),
        ),
        check_vma=False,
    )
```

profile of v0, /device:TPU:1, one launch (start us, length us, event | category | flops | bytes accessed | tf_op | source)
XLA Modules:
  0.0 170.2 jit_solution(17979015256726700255)
XLA Ops:
  0.6 0.0 copy-start
  1.5 8.0 %fusion.11 = bf16[768,2048]{1,0:T(8,128)(2,1)} fusion(bf16[1,1024,2048]{2,1,0:T(8,128)(2,1)} %param.10, pred[1024]{0:T(1024)(128)(4,1)S(1)} %iota_compare_fusion.2, bf16[1,1024,768]{2,1,0:T(8,128)(2,1)} %param.9), kind=kOutput, calls=%fused_computation.15 | convolution fusion | flops 3224895488 | bytes 8913920 | tf_op jit(solution)/shard_map/dot_general | solution.py:16
  9.5 6.3 %all_to_all.10 = bf16[128,6,2048]{2,1,0:T(8,128)(2,1)} reshape(bf16[768,2048]{1,0:T(8,128)(2,1)} %fusion.11) | data formatting | bytes 6291456 | tf_op jit(solution)/shard_map/all_to_all | solution.py:46
  15.8 0.0 copy-start.1
  15.8 0.0 copy-start.2
  15.8 11.9 %all-to-all-start = ((bf16[128,6,2048]{2,1,0:T(8,128)(2,1)}), bf16[128,6,2048]{2,1,0:T(8,128)(2,1)}, u32[]{:S(2)}, u32[]{:S(2)}) async-start(bf16[128,6,2048]{2,1,0:T(8,128)(2,1)} %all_to_all.10), calls=%async_computation | async-start | bytes 8388608 | tf_op jit(solution)/shard_map/all_to_all | solution.py:46
  27.7 0.0 copy-done.1
  27.7 0.1 copy.22
  27.8 0.1 reduce-window.8
  27.9 0.1 reduce
  28.0 0.0 copy-done.2
  28.1 0.1 convert_reduce_fusion
  28.2 52.1 %all-to-all-done = bf16[128,6,2048]{2,1,0:T(8,128)(2,1)} async-done(((bf16[128,6,2048]{2,1,0:T(8,128)(2,1)}), bf16[128,6,2048]{2,1,0:T(8,128)(2,1)}, u32[]{:S(2)}, u32[]{:S(2)}) %all-to-all-start) | async-done | bytes 3145760 | tf_op jit(solution)/shard_map/all_to_all | solution.py:46
  80.2 13.9 %fusion.32 = (bf16[64,6,2048]{2,0,1:T(8,128)(2,1)S(1)}, f32[64,6,2048]{2,0,1:T(8,128)}, bf16[64,6,2048]{2,0,1:T(8,128)(2,1)}, bf16[64,6,2048]{2,0,1:T(8,128)(2,1)}) fusion(f32[64,6,2048]{2,0,1:T(8,128)} %param.15, bf16[64,6,2048]{2,0,1:T(8,128)(2,1)} %param.17, bf16[64,6,2048]{2,0,1:T(8,128)(2,1)} %param.16, bf16[128,6,2048]{2,1,0:T(8,128)(2,1)} %all-to-all-done, ...), kind=kOutput, calls=%fused_computation.32 | convolution fusion | flops 217063424 | bytes 17302016 | tf_op jit(solution)/shard_map/es,src->erc/dot_general | solution.py:49
  94.1 2.2 %copy.24 = bf16[64,6,2048]{2,1,0:T(8,128)(2,1)} copy(bf16[64,6,2048]{2,0,1:T(8,128)(2,1)S(1)} %get-tuple-element.5) | data formatting | bytes 3145728 | tf_op jit(solution)/shard_map/convert_element_type | solution.py:59
  96.3 4.4 %gather_fusion = bf16[128,6,2048]{2,1,0:T(8,128)(2,1)} fusion(bf16[64,6,2048]{2,1,0:T(8,128)(2,1)} %copy.24, s32[1024]{0:T(1024)S(1)} %pad_clamp_fusion), kind=kCustom, calls=%fused_computation | custom fusion | bytes 6291968 | tf_op jit(solution)/shard_map/jit(_take)/gather | solution.py:59
  100.7 4.7 %broadcast_select_fusion = bf16[128,6,2048]{2,1,0:T(8,128)(2,1)} fusion(bf16[128,6,2048]{2,1,0:T(8,128)(2,1)} %gather_fusion, pred[128]{0:T(512)(128)(4,1)S(1)} %compare_and_fusion), kind=kLoop, calls=%fused_computation.6 | loop fusion | flops 1572864 | bytes 6291584 | tf_op jit(solution)/shard_map/jit(_take)/select_n | solution.py:59
  105.4 6.0 %all-to-all-start.1 = ((bf16[128,6,2048]{2,1,0:T(8,128)(2,1)}), bf16[128,6,2048]{2,1,0:T(8,128)(2,1)}, u32[]{:S(2)}, u32[]{:S(2)}) async-start(bf16[128,6,2048]{2,1,0:T(8,128)(2,1)} %broadcast_select_fusion), calls=%async_computation.1 | async-start | bytes 8388608 | tf_op jit(solution)/shard_map/all_to_all | solution.py:62
  111.4 0.0 copy-done
  111.4 6.8 %fusion.22 = bf16[1,1024,768]{2,1,0:T(8,128)(2,1)} fusion(bf16[1,768,2048]{2,1,0:T(8,128)(2,1)S(1)} %copy-done, bf16[1,1024,2048]{2,1,0:T(8,128)(2,1)} %param.10, pred[1024]{0:T(1024)(128)(4,1)S(1)} %iota_compare_fusion.2), kind=kOutput, calls=%fused_computation.20 | convolution fusion | flops 3224109056 | bytes 8913920 | tf_op jit(solution)/shard_map/dot_general | solution.py:22
  118.2 45.7 %all-to-all-done.1 = bf16[128,6,2048]{2,1,0:T(8,128)(2,1)} async-done(((bf16[128,6,2048]{2,1,0:T(8,128)(2,1)}), bf16[128,6,2048]{2,1,0:T(8,128)(2,1)}, u32[]{:S(2)}, u32[]{:S(2)}) %all-to-all-start.1) | async-done | bytes 3145760 | tf_op jit(solution)/shard_map/all_to_all | solution.py:62
  163.9 6.3 %broadcast_in_dim.40 = bf16[1,768,2048]{2,1,0:T(8,128)(2,1)} reshape(bf16[128,6,2048]{2,1,0:T(8,128)(2,1)} %all-to-all-done.1) | data formatting | bytes 6291456 | tf_op jit(solution)/shard_map/broadcast_in_dim | solution.py:68
  (4 shorter events, 0.0 us)
Async XLA Ops:
  0.6 110.8 %copy-start = (bf16[1,768,2048]{2,1,0:T(8,128)(2,1)S(1)}, bf16[1,768,2048]{2,1,0:T(8,128)(2,1)}, u32[]{:S(2)}) copy-start(bf16[1,768,2048]{2,1,0:T(8,128)(2,1)} %param.11) | copy-start | bytes 9437188
  15.8 12.0 %copy-start.1 = (s32[64]{0:T(128)S(1)}, s32[64]{0:T(128)}, u32[]{:S(2)}) copy-start(s32[64]{0:T(128)} %param.12) | copy-start | bytes 772
  15.8 12.3 %copy-start.2 = (s32[128]{0:T(128)S(1)}, s32[128]{0:T(128)}, u32[]{:S(2)}) copy-start(s32[128]{0:T(128)} %param.14) | copy-start | bytes 1540
  15.8 64.5 %all-to-all-start = ((bf16[128,6,2048]{2,1,0:T(8,128)(2,1)}), bf16[128,6,2048]{2,1,0:T(8,128)(2,1)}, u32[]{:S(2)}, u32[]{:S(2)}) async-start(bf16[128,6,2048]{2,1,0:T(8,128)(2,1)} %all_to_all.10), calls=%async_computation | async-start | bytes 8388608 | tf_op jit(solution)/shard_map/all_to_all | solution.py:46
  105.4 58.5 %all-to-all-start.1 = ((bf16[128,6,2048]{2,1,0:T(8,128)(2,1)}), bf16[128,6,2048]{2,1,0:T(8,128)(2,1)}, u32[]{:S(2)}, u32[]{:S(2)}) async-start(bf16[128,6,2048]{2,1,0:T(8,128)(2,1)} %broadcast_select_fusion), calls=%async_computation.1 | async-start | bytes 8388608 | tf_op jit(solution)/shard_map/all_to_all | solution.py:62
where the time goes:
time: 171 us; the launch traced here: 170 us
  waiting for transfers between devices  97.7 us (57%)
  matrix products  28.7 us (17%)
  local copies, waits for them, and re-layouts  19.3 us (11%)
  starting transfers between devices  18 us (11%)
  other arithmetic  5.02 us (3%)
    all_to_all x1, waiting for transfers between devices, per_device(): lax.all_to_all(slot_grads, 'dev', split_axis=0, concat_axis=0, tiled=True)  52.1 us
    all_to_all x1, waiting for transfers between devices, per_device(): lax.all_to_all(outgoing, 'dev', split_axis=0, concat_axis=0, tiled=True)  45.7 us
    dot_general x1, matrix products, per_device(): jnp.einsum('es,src->erc', selector, pieces, preferred_element_type=jnp.fl...  13.9 us
    all_to_all x1, starting transfers between devices, per_device(): lax.all_to_all(slot_grads, 'dev', split_axis=0, concat_axis=0, tiled=True)  11.9 us
    dot_general x1, matrix products, contract_rows(): lax.dot_general(left, right, (((0,), (0,)), ((), ())), preferred_element_...  8.04 us
    dot_general x1, matrix products, contract_cols(): lax.dot_general(left, right, (((1,), (1,)), ((), ())), preferred_element_...  6.8 us
    broadcast_in_dim x1, local copies, waits for them, and re-layouts, per_device(): arriving[None]  6.32 us
    all_to_all x1, local copies, waits for them, and re-layouts, per_device(): lax.all_to_all(slot_grads, 'dev', split_axis=0, concat_axis=0, tiled=True)  6.26 us
  transfers between devices with their start and end apart: 2, of which 2 were waited for; matrix products, arithmetic and copies ran while one was open for 4% of the time, Pallas kernels for 0%

commit v1 on v0

v1 whole, which is shorter than its diff:
```python
import functools
import jax
import jax.numpy as jnp
from jax import lax
from jax.experimental import pallas as pl
from jax.experimental.pallas import tpu as pltpu
from jax.sharding import PartitionSpec as P

LEARN_RATE = 0.001
DECAY_RATE = 0.1
BETA_ONE = 0.9
BETA_TWO = 0.95
BIAS_ONE = 1.0 - 0.9**20
BIAS_TWO = 1.0 - 0.95**20
EPSILON = 1e-08

LANES = 128
GROUP = 4


def contract_cols(left, right):
    return lax.dot_general(
        left, right, (((1,), (1,)), ((), ())), preferred_element_type=jnp.float32
    )


def grads_kernel(live_ref, saved_ref, cot_ref, out_ref, turned, sums, chunk):
    step = pl.program_id(0)
    rows, hidden = saved_ref.shape
    blocks = sums.shape[0]
    wide = cot_ref.shape[1]
    per_step = wide // LANES
    devices = out_ref.shape[0]
    share = hidden // devices

    @pl.when(step == 0)
    def _():
        index = lax.broadcasted_iota(jnp.int32, (rows, hidden), 0)
        kept = jnp.where(index < live_ref[0], saved_ref[...], jnp.zeros_like(saved_ref))
        turned[...] = kept.T

    product = jnp.dot(turned[...], cot_ref[...], preferred_element_type=jnp.float32)
    for part in range(per_step):
        sums[step * per_step + part] = product[:, part * LANES : (part + 1) * LANES]

    @pl.when(step == pl.num_programs(0) - 1)
    def _():
        @pl.loop(0, devices // GROUP)
        def _(group):
            base = pl.multiple_of(group * GROUP * share, 8)
            tall = GROUP * share
            for block in range(blocks):
                piece = sums[block, pl.ds(base, tall), :]
                for member in range(GROUP):
                    chunk[member, block * share : (block + 1) * share, :] = piece[
                        member * share : (member + 1) * share, :
                    ]
            for member in range(GROUP):
                out_ref[group * GROUP + member] = chunk[member].astype(jnp.bfloat16)


def slot_chunks(saved, cot, live, devices):
    rows, hidden = saved.shape
    width = cot.shape[1]
    wide = 2 * LANES
    share = hidden // devices
    blocks = width // LANES
    return pl.pallas_call(
        grads_kernel,
        out_shape=jax.ShapeDtypeStruct((devices, blocks * share, LANES), jnp.bfloat16),
        grid_spec=pltpu.PrefetchScalarGridSpec(
            num_scalar_prefetch=1,
            grid=(width // wide,),
            in_specs=[
                pl.BlockSpec((rows, hidden), lambda n, live: (0, 0), pipeline_mode=pl.Buffered(1)),
                pl.BlockSpec((rows, wide), lambda n, live: (0, n)),
            ],
            out_specs=pl.BlockSpec((devices, blocks * share, LANES), lambda n, live: (0, 0, 0)),
            scratch_shapes=[
                pltpu.VMEM((hidden, rows), jnp.bfloat16),
                pltpu.VMEM((blocks, hidden, LANES), jnp.float32),
                pltpu.VMEM((GROUP, blocks * share, LANES), jnp.float32),
            ],
        ),
        compiler_params=pltpu.CompilerParams(
            dimension_semantics=("arbitrary",), vmem_limit_bytes=40 << 20
        ),
        cost_estimate=pl.CostEstimate(
            flops=2 * rows * hidden * width,
            bytes_accessed=2 * (rows * hidden + rows * width + hidden * width),
            transcendentals=0,
        ),
        name="slot_chunks",
    )(live, saved, cot)


def adam_kernel(
    holder_ref, fresh_ref, next_ref, pieces_ref, master_ref, one_ref, two_ref,
    master_out, one_out, two_out, send_out,
    grads, master_in, one_in, two_in, new_master, new_one, new_two, ready, load_sem, store_sem, send_sem,
):
    slots, height, _ = pieces_ref.shape
    share, experts, width = master_ref.shape
    blocks = width // LANES

    def loads(row):
        return (
            pltpu.make_async_copy(master_ref.at[row], master_in.at[row], load_sem.at[0, row]),
            pltpu.make_async_copy(one_ref.at[row], one_in.at[row], load_sem.at[1, row]),
            pltpu.make_async_copy(two_ref.at[row], two_in.at[row], load_sem.at[2, row]),
        )

    def stores(row):
        return (
            pltpu.make_async_copy(new_master.at[row], master_out.at[row], store_sem.at[0, row]),
            pltpu.make_async_copy(new_one.at[row], one_out.at[row], store_sem.at[1, row]),
            pltpu.make_async_copy(new_two.at[row], two_out.at[row], store_sem.at[2, row]),
        )

    for row in range(share):
        for copy in loads(row):
            copy.start()

    def add_slot(slot, total):
        total = jnp.where(fresh_ref[slot] > 0, 0.0, total) + pieces_ref[slot].astype(jnp.float32)
        grads[pl.ds(holder_ref[slot], height, stride=experts), :] = total
        return total

    lax.fori_loop(0, slots, add_slot, jnp.zeros((height, LANES), jnp.float32), unroll=4)

    for row in range(share):
        for copy in loads(row):
            copy.wait()

        @pl.loop(0, blocks)
        def _(block):
            lanes = pl.ds(pl.multiple_of(block * LANES, LANES), LANES)
            place = pl.ds(pl.multiple_of((block * share + row) * experts, experts), experts)
            grad = grads[place, :]
            old = master_in[row, :, lanes]
            first = BETA_ONE * one_in[row, :, lanes].astype(jnp.float32) + (1.0 - BETA_ONE) * grad
            second = (
                BETA_TWO * two_in[row, :, lanes].astype(jnp.float32)
                + (1.0 - BETA_TWO) * grad * grad
            )
            update = (
                first * (1.0 / BIAS_ONE) / (jnp.sqrt(second * (1.0 / BIAS_TWO)) + EPSILON)
                + DECAY_RATE * old
            )
            new = old - LEARN_RATE * update
            new_master[row, :, lanes] = new
            new_one[row, :, lanes] = first.astype(jnp.bfloat16)
            new_two[row, :, lanes] = second.astype(jnp.bfloat16)
            grads[place, :] = new

        for copy in stores(row):
            copy.start()

    @pl.loop(0, experts)
    def _(expert):
        ready[expert] = grads[pl.ds(expert, height, stride=experts), :].astype(jnp.bfloat16)

    @pl.loop(0, slots)
    def _(slot):
        pltpu.make_async_copy(ready.at[next_ref[slot]], send_out.at[slot], send_sem.at[0]).start()

    for row in range(share):
        for copy in stores(row):
            copy.wait()
    pltpu.make_async_copy(send_out, send_out, send_sem.at[0]).wait()


def adam_step(holder, fresh, next_map, pieces, master, one, two):
    slots, height, _ = pieces.shape
    share, experts, width = master.shape
    space = pl.BlockSpec(memory_space=pl.ANY)
    return pl.pallas_call(
        adam_kernel,
        out_shape=(
            jax.ShapeDtypeStruct(master.shape, jnp.float32),
            jax.ShapeDtypeStruct(one.shape, jnp.bfloat16),
            jax.ShapeDtypeStruct(two.shape, jnp.bfloat16),
            jax.ShapeDtypeStruct((slots, height, LANES), jnp.bfloat16),
        ),
        grid_spec=pltpu.PrefetchScalarGridSpec(
            num_scalar_prefetch=3,
            grid=(1,),
            in_specs=[
                pl.BlockSpec(pieces.shape, lambda i, *s: (0, 0, 0), pipeline_mode=pl.Buffered(1)),
                space, space, space,
            ],
            out_specs=(space, space, space, space),
            scratch_shapes=[
                pltpu.VMEM((height * experts, LANES), jnp.float32),
                pltpu.VMEM(master.shape, jnp.float32),
                pltpu.VMEM(one.shape, jnp.bfloat16),
                pltpu.VMEM(two.shape, jnp.bfloat16),
                pltpu.VMEM(master.shape, jnp.float32),
                pltpu.VMEM(one.shape, jnp.bfloat16),
                pltpu.VMEM(two.shape, jnp.bfloat16),
                pltpu.VMEM((experts, height, LANES), jnp.bfloat16),
                pltpu.SemaphoreType.DMA((3, share)),
                pltpu.SemaphoreType.DMA((3, share)),
                pltpu.SemaphoreType.DMA((1,)),
            ],
        ),
        compiler_params=pltpu.CompilerParams(
            dimension_semantics=("arbitrary",), vmem_limit_bytes=40 << 20
        ),
        name="adam_step",
    )(holder, fresh, next_map, pieces, master, one, two)


def rows_kernel(in_ref, out_ref, chunk, tall):
    groups = in_ref.shape[0] // GROUP
    width = out_ref.shape[1]
    blocks = width // LANES
    share = in_ref.shape[1] // blocks
    height = GROUP * share

    @pl.loop(0, groups)
    def _(group):
        for member in range(GROUP):
            chunk[member] = in_ref[group * GROUP + member].astype(jnp.float32)
        base = pl.multiple_of(group * height, 8)
        for block in range(blocks):
            for member in range(GROUP):
                tall[block, member * share : (member + 1) * share, :] = chunk[
                    member, block * share : (block + 1) * share, :
                ]
            out_ref[pl.ds(base, height), block * LANES : (block + 1) * LANES] = tall[
                block
            ].astype(jnp.bfloat16)


def chunk_rows(arrived, hidden, width, steps=8):
    slots, height, _ = arrived.shape
    blocks = width // LANES
    share = height // blocks
    return pl.pallas_call(
        rows_kernel,
        out_shape=jax.ShapeDtypeStruct((hidden, width), jnp.bfloat16),
        grid=(steps,),
        in_specs=[pl.BlockSpec((slots // steps, height, LANES), lambda i: (i, 0, 0))],
        out_specs=pl.BlockSpec((hidden // steps, width), lambda i: (i, 0)),
        scratch_shapes=[
            pltpu.VMEM((GROUP, height, LANES), jnp.float32),
            pltpu.VMEM((blocks, GROUP * share, LANES), jnp.float32),
        ],
        compiler_params=pltpu.CompilerParams(
            dimension_semantics=("arbitrary",), vmem_limit_bytes=20 << 20
        ),
        name="chunk_rows",
    )(arrived)


def exchange(chunks):
    return lax.all_to_all(chunks, "dev", split_axis=0, concat_axis=0, tiled=True)


def per_device(saved, cotangent, weights, counts, live_rows, next_map, master, moment1, moment2):
    cot_rows = cotangent[0]
    devices = lax.axis_size("dev")
    experts, share, width = master.shape
    hidden = saved.shape[2]
    row_count = saved.shape[1]
    chunks = slot_chunks(saved[0], cot_rows, live_rows, devices)
    received = exchange(chunks)
    row_index = jnp.arange(row_count, dtype=jnp.int32)
    masked = jnp.where(
        (row_index < live_rows[0])[:, None], cot_rows, jnp.zeros_like(cot_rows)
    )
    input_grads = contract_cols(masked, weights[0]).astype(jnp.bfloat16)
    slot_index = jnp.arange(devices, dtype=jnp.int32)
    bounds = jnp.cumsum(counts)
    holders = jnp.sum((bounds[None, :] <= slot_index[:, None]).astype(jnp.int32), axis=1)
    fresh = jnp.any(bounds[None, :] == slot_index[:, None], axis=1) | (slot_index == 0)
    new_master, new_one, new_two, outgoing = adam_step(
        holders, fresh.astype(jnp.int32), next_map, received,
        master.transpose(1, 0, 2), moment1.transpose(1, 0, 2), moment2.transpose(1, 0, 2),
    )
    arriving = exchange(outgoing)
    next_weights = chunk_rows(arriving, hidden, width)
    return (
        input_grads[None],
        new_master.transpose(1, 0, 2),
        new_one.transpose(1, 0, 2),
        new_two.transpose(1, 0, 2),
        next_weights[None],
    )


def solution(mesh):
    placed = (
        P("dev", None, None),
        P("dev", None, None),
        P("dev", None, None),
        P(),
        P("dev"),
        P(),
        P(None, "dev", None),
        P(None, "dev", None),
        P(None, "dev", None),
    )
    return jax.shard_map(
        per_device,
        mesh=mesh,
        in_specs=placed,
        out_specs=(
            P("dev", None, None),
            P(None, "dev", None),
            P(None, "dev", None),
            P(None, "dev", None),
            P("dev", None, None),
        ),
        check_vma=False,
    )
```

time: 171 us -> 151 us (0.88)
  Pallas kernels: 0 us -> 36.6 us
  waiting for transfers between devices: 97.7 us -> 75.4 us
  matrix products: 28.7 us -> 6.8 us
  local copies, waits for them, and re-layouts: 19.3 us -> 11.9 us
  other arithmetic: 5.02 us -> 0.41 us
    pallas_call x0 -> x3, Pallas kernels: none -> 36.6 us  [the longest x1 22.7 us: adam_step(): pl.pallas_call(adam_kernel, out_shape=(jax.ShapeDtypeStruct(master.shape,...]
    all_to_all x2, waiting for transfers between devices: 97.7 us -> 75.4 us  [exchange(): lax.all_to_all(chunks, 'dev', split_axis=0, concat_axis=0, tiled=True)]
    dot_general x2 -> x0, matrix products: 21.9 us -> none  [the longest x1 13.9 us: per_device(): jnp.einsum('es,src->erc', selector, pieces, preferred_element_type=jnp.fl...]
    unnamed x6 -> x20, local copies, waits for them, and re-layouts: 0.02 us -> 11.8 us
    broadcast_in_dim x1 -> x0, local copies, waits for them, and re-layouts: 6.32 us -> none  [per_device(): arriving[None]]
    all_to_all x1 -> x0, local copies, waits for them, and re-layouts: 6.26 us -> none  [per_device(): lax.all_to_all(slot_grads, 'dev', split_axis=0, concat_axis=0, tiled=True)]
    select_n x2 -> x0, other arithmetic: 4.7 us -> none  [per_device(): jnp.take(master_out.astype(jnp.bfloat16), next_map, axis=0)]
    gather x1 -> x0, local copies, waits for them, and re-layouts: 4.37 us -> none  [per_device(): jnp.take(master_out.astype(jnp.bfloat16), next_map, axis=0)]
  transfers between devices with their start and end apart: 2 -> 2, of which waited for: 2 -> 2; matrix products, arithmetic and copies ran while one was open for 4% -> 5% of each run, Pallas kernels for 0% -> 0%
where the time goes in v1:
time: 151 us; the launch traced here: 150 us
  waiting for transfers between devices  75.4 us (50%)
  Pallas kernels  36.6 us (24%)
  starting transfers between devices  17.5 us (12%)
  local copies, waits for them, and re-layouts  11.9 us (8%)
  matrix products  6.8 us (5%)
  between operations  1.54 us (1%)
    all_to_all x2, waiting for transfers between devices, exchange(): lax.all_to_all(chunks, 'dev', split_axis=0, concat_axis=0, tiled=True)  75.4 us
    pallas_call x1, Pallas kernels, adam_step(): pl.pallas_call(adam_kernel, out_shape=(jax.ShapeDtypeStruct(master.shape,...  22.7 us
    all_to_all x2, starting transfers between devices, exchange(): lax.all_to_all(chunks, 'dev', split_axis=0, concat_axis=0, tiled=True)  17.5 us
    unnamed x20, local copies, waits for them, and re-layouts  11.8 us
    pallas_call x1, Pallas kernels, slot_chunks(): pl.pallas_call(grads_kernel, out_shape=jax.ShapeDtypeStruct((devices, blo...  7.07 us
    pallas_call x1, Pallas kernels, chunk_rows(): pl.pallas_call(rows_kernel, out_shape=jax.ShapeDtypeStruct((hidden, width...  6.82 us
    dot_general x1, matrix products, contract_cols(): lax.dot_general(left, right, (((1,), (1,)), ((), ())), preferred_element_...  6.8 us
  transfers between devices with their start and end apart: 2, of which 2 were waited for; matrix products, arithmetic and copies ran while one was open for 5% of the time, Pallas kernels for 0%

profile of v1, /device:TPU:1, one launch (start us, length us, event | category | flops | bytes accessed | tf_op | source)
XLA Modules:
  0.0 150.1 jit_solution(1474608140392383010)
XLA Ops:
  0.6 0.0 copy-start
  1.4 0.0 copy-start.7
  1.5 2.3 %copy-done.7 = bf16[1,1024,2048]{2,1,0:T(8,128)(2,1)S(1)} copy-done((bf16[1,1024,2048]{2,1,0:T(8,128)(2,1)S(1)}, bf16[1,1024,2048]{2,1,0:T(8,128)(2,1)}, u32[]{:S(2)}) %copy-start.7) | copy-done | bytes 4194328
  3.8 0.0 copy-start.8
  3.8 1.4 copy-done.8
  5.2 7.1 %slot_chunks.1 = bf16[128,96,128]{2,1,0:T(8,128)(2,1)S(1)} custom-call(s32[1]{0:T(128)} %copy.17.live_ref, bf16[1024,768]{1,0:T(8,128)(2,1)S(1)} %bitcast.32, bf16[1024,2048]{1,0:T(8,128)(2,1)S(1)} %bitcast.31), custom_call_target="tpu_custom_call" | custom-call | flops 3221225472 | bytes 8912896 | tf_op jit(solution)/shard_map/slot_chunks/pallas_call | solution.py:68
  12.3 0.0 copy-start.2
  12.3 1.7 %copy-done.2 = bf16[128,96,128]{2,1,0:T(8,128)(2,1)} copy-done((bf16[128,96,128]{2,1,0:T(8,128)(2,1)}, bf16[128,96,128]{2,1,0:T(8,128)(2,1)S(1)}, u32[]{:S(2)}) %copy-start.2) | copy-done | bytes 3145752
  13.9 0.0 copy-start.9
  13.9 0.0 copy-start.6
  13.9 11.9 %all-to-all-start = ((bf16[128,96,128]{2,1,0:T(8,128)(2,1)}), bf16[128,96,128]{2,1,0:T(8,128)(2,1)}, u32[]{:S(2)}, u32[]{:S(2)}) async-start(bf16[128,96,128]{2,1,0:T(8,128)(2,1)} %copy-done.2), calls=%async_computation | async-start | bytes 6291456 | tf_op jit(solution)/shard_map/all_to_all | solution.py:258
  25.8 0.0 copy-done.9
  25.9 0.1 copy.16
  26.0 0.1 reduce-window.8
  26.0 0.1 reduce
  26.2 0.1 fusion.16
  26.3 0.1 convert_reduce_fusion.holder_ref
  26.4 40.8 %all-to-all-done.pieces_ref = bf16[128,96,128]{2,1,0:T(8,128)(2,1)} async-done(((bf16[128,96,128]{2,1,0:T(8,128)(2,1)}), bf16[128,96,128]{2,1,0:T(8,128)(2,1)}, u32[]{:S(2)}, u32[]{:S(2)}) %all-to-all-start) | async-done | bytes 3145760 | tf_op jit(solution)/shard_map/all_to_all | solution.py:258
  67.1 0.0 copy-done.6
  67.1 0.0 copy-start.1
  67.1 1.9 %copy-done.1 = f32[64,6,2048]{2,0,1:T(8,128)S(1)} copy-done((f32[64,6,2048]{2,0,1:T(8,128)S(1)}, f32[64,6,2048]{2,0,1:T(8,128)}, u32[]{:S(2)}) %copy-start.1) | copy-done | bytes 3145752
  69.0 0.0 copy-start.4
  69.0 1.4 copy-done.4
  70.4 0.0 copy-start.5
  70.4 1.4 copy-done.5
  71.9 22.7 %adam_step.1 = (f32[6,64,2048]{2,1,0:T(8,128)}, bf16[6,64,2048]{2,1,0:T(8,128)(2,1)}, bf16[6,64,2048]{2,1,0:T(8,128)(2,1)}, bf16[128,96,128]{2,1,0:T(8,128)(2,1)S(1)}) custom-call(s32[128]{0:T(128)S(1)} %convert_reduce_fusion.holder_ref, s32[128]{0:T(128)S(1)} %or_convert_fusion.fresh_ref, s32[128]{0:T(128)S(1)} %copy-done.6, ...), custom_call_target="tpu_custom_call" | custom-call | tf_op jit(solution)/shard_map/adam_step/pallas_call | solution.py:177
  94.6 0.0 copy-start.3
  94.6 1.7 %copy-done.3 = bf16[128,96,128]{2,1,0:T(8,128)(2,1)} copy-done((bf16[128,96,128]{2,1,0:T(8,128)(2,1)}, bf16[128,96,128]{2,1,0:T(8,128)(2,1)S(1)}, u32[]{:S(2)}) %copy-start.3) | copy-done | bytes 3145752
  96.3 5.6 %all-to-all-start.1 = ((bf16[128,96,128]{2,1,0:T(8,128)(2,1)}), bf16[128,96,128]{2,1,0:T(8,128)(2,1)}, u32[]{:S(2)}, u32[]{:S(2)}) async-start(bf16[128,96,128]{2,1,0:T(8,128)(2,1)} %copy-done.3), calls=%async_computation.1 | async-start | bytes 6291456 | tf_op jit(solution)/shard_map/all_to_all | solution.py:258
  101.9 0.0 copy-done
  101.9 6.8 %fusion.11 = bf16[1,1024,768]{2,1,0:T(8,128)(2,1)} fusion(bf16[1,768,2048]{2,1,0:T(8,128)(2,1)S(1)} %copy-done, bf16[1,1024,2048]{2,1,0:T(8,128)(2,1)} %param.10, pred[1024]{0:T(1024)(128)(4,1)S(1)} %iota_compare_fusion.2), kind=kOutput, calls=%fused_computation.7 | convolution fusion | flops 3224109056 | bytes 8913920 | tf_op jit(solution)/shard_map/dot_general | solution.py:22
  108.7 34.6 %all-to-all-done.1.in_ref = bf16[128,96,128]{2,1,0:T(8,128)(2,1)} async-done(((bf16[128,96,128]{2,1,0:T(8,128)(2,1)}), bf16[128,96,128]{2,1,0:T(8,128)(2,1)}, u32[]{:S(2)}, u32[]{:S(2)}) %all-to-all-start.1) | async-done | bytes 3145760 | tf_op jit(solution)/shard_map/all_to_all | solution.py:258
  143.3 6.8 %chunk_rows.1 = bf16[768,2048]{1,0:T(8,128)(2,1)} custom-call(bf16[128,96,128]{2,1,0:T(8,128)(2,1)} %all-to-all-done.1.in_ref), custom_call_target="tpu_custom_call" | custom-call | tf_op jit(solution)/shard_map/chunk_rows/pallas_call | solution.py:240
  (2 shorter events, 0.0 us)
Async XLA Ops:
  0.6 101.3 %copy-start = (bf16[1,768,2048]{2,1,0:T(8,128)(2,1)S(1)}, bf16[1,768,2048]{2,1,0:T(8,128)(2,1)}, u32[]{:S(2)}) copy-start(bf16[1,768,2048]{2,1,0:T(8,128)(2,1)} %param.11) | copy-start | bytes 9437188
  1.4 2.3 %copy-start.7 = (bf16[1,1024,2048]{2,1,0:T(8,128)(2,1)S(1)}, bf16[1,1024,2048]{2,1,0:T(8,128)(2,1)}, u32[]{:S(2)}) copy-start(bf16[1,1024,2048]{2,1,0:T(8,128)(2,1)} %param.10) | copy-start | bytes 12582916
  3.8 1.4 copy-start.8
  12.3 1.7 %copy-start.2 = (bf16[128,96,128]{2,1,0:T(8,128)(2,1)}, bf16[128,96,128]{2,1,0:T(8,128)(2,1)S(1)}, u32[]{:S(2)}) copy-start(bf16[128,96,128]{2,1,0:T(8,128)(2,1)S(1)} %slot_chunks.1) | copy-start | bytes 9437188
  13.9 11.9 %copy-start.9 = (s32[64]{0:T(128)S(1)}, s32[64]{0:T(128)}, u32[]{:S(2)}) copy-start(s32[64]{0:T(128)} %param.12) | copy-start | bytes 772
  13.9 53.2 %copy-start.6 = (s32[128]{0:T(128)S(1)}, s32[128]{0:T(128)}, u32[]{:S(2)}) copy-start(s32[128]{0:T(128)} %next_ref.1) | copy-start | bytes 1540
  13.9 53.2 %all-to-all-start = ((bf16[128,96,128]{2,1,0:T(8,128)(2,1)}), bf16[128,96,128]{2,1,0:T(8,128)(2,1)}, u32[]{:S(2)}, u32[]{:S(2)}) async-start(bf16[128,96,128]{2,1,0:T(8,128)(2,1)} %copy-done.2), calls=%async_computation | async-start | bytes 6291456 | tf_op jit(solution)/shard_map/all_to_all | solution.py:258
  67.1 1.9 %copy-start.1 = (f32[64,6,2048]{2,0,1:T(8,128)S(1)}, f32[64,6,2048]{2,0,1:T(8,128)}, u32[]{:S(2)}) copy-start(f32[64,6,2048]{2,0,1:T(8,128)} %param.15) | copy-start | bytes 9437188
  69.0 1.4 copy-start.4
  70.4 1.4 copy-start.5
  94.6 1.7 %copy-start.3 = (bf16[128,96,128]{2,1,0:T(8,128)(2,1)}, bf16[128,96,128]{2,1,0:T(8,128)(2,1)S(1)}, u32[]{:S(2)}) copy-start(bf16[128,96,128]{2,1,0:T(8,128)(2,1)S(1)} %get-tuple-element.12) | copy-start | bytes 9437188
  96.3 47.1 %all-to-all-start.1 = ((bf16[128,96,128]{2,1,0:T(8,128)(2,1)}), bf16[128,96,128]{2,1,0:T(8,128)(2,1)}, u32[]{:S(2)}, u32[]{:S(2)}) async-start(bf16[128,96,128]{2,1,0:T(8,128)(2,1)} %copy-done.3), calls=%async_computation.1 | async-start | bytes 6291456 | tf_op jit(solution)/shard_map/all_to_all | solution.py:258
